TPU v7x, 256 devices: a whole 4x4x8 slice. The times are simulated.
256 devices in a mesh: frames: 32 (over y, z_lo, x), space: 8 (over z_hi, core).
Axes of the slice: x: 4, y: 4, z: 8 (z_hi: 4, z_lo: 2; z = z_hi * 2 + z_lo), core: 2. Of those that a mesh axis runs over, the one named last changes fastest.
Arguments:
- latents: bfloat16 [32, 3584, 1152], P('frames', 'space'), may hold values from -6 to 6
- merge_slot: int32 [32, 3584], P('frames', 'space'), may hold values from 0 to 1791, as said below
- modulation: float32 [6, 1152], replicated, may hold values from -3 to 3
- spatial_qkv: bfloat16 [1152, 1728], replicated, may hold values from -0.41247896 to 0.41247896
- spatial_proj: bfloat16 [576, 1152], replicated, may hold values from -0.25 to 0.25
- temporal_qkv: bfloat16 [1152, 1728], replicated, may hold values from -0.41247896 to 0.41247896
- temporal_proj: bfloat16 [576, 1152], replicated, may hold values from -0.25 to 0.25
Outputs:
- block_out: bfloat16 [32, 3584, 1152], P('frames', 'space')
Inputs may be any that keep to these rules, and one draw needn't show every extreme that they name: `merge_slot`: within each frame, the tokens of the k-th aligned block of 448 tokens join merged tokens k * 224 to (k + 1) * 224 - 1 only, and every merged token is joined by at least one token.
All inputs are finite; a program needn't handle non-finite values.
Results may differ from a plain program's by a relative error of at most 0.0062.
Values may be sent and summed in bfloat16 or wider, within the bound.
A program may use at most 128 MiB of HBM per device.

v0:
```python
import math
import jax
import jax.numpy as jnp
from jax import lax
from jax.sharding import PartitionSpec as P

HEADS = 8
HD = 72


def layer_norm(values):
    values = values.astype(jnp.float32)
    center = values - jnp.mean(values, -1, keepdims=True)
    spread = jnp.mean(center * center, -1, keepdims=True)
    return center * lax.rsqrt(spread + 1e-06)


def modulate(values, modulation, which):
    return (layer_norm(values) * (1.0 + modulation[which + 1]) + modulation[which]).astype(
        jnp.bfloat16
    )


def shards(latents, merge_slot, modulation, spatial_qkv, spatial_proj, temporal_qkv, temporal_proj):
    row_count = latents.shape[1]
    slot_count = row_count // 2
    width = latents.shape[2]
    inner = spatial_proj.shape[0]
    root_size = math.sqrt(HD)
    own_rows = latents[0]
    normed = modulate(own_rows, modulation, 0)
    local_slot = merge_slot[0] - lax.axis_index("space") * slot_count
    one_hot = (local_slot[:, None] == jnp.arange(slot_count, dtype=jnp.int32)[None, :]).astype(
        jnp.bfloat16
    )
    counts = jnp.sum(one_hot.astype(jnp.float32), 0)
    summed = lax.dot_general(
        one_hot, normed, (((0,), (0,)), ((), ())), preferred_element_type=jnp.float32
    )
    merged = (summed / counts[:, None]).astype(jnp.bfloat16)
    projected = jnp.dot(merged, spatial_qkv, preferred_element_type=jnp.float32).astype(
        jnp.bfloat16
    )
    query_rows = projected[:, :inner]
    key_rows = projected[:, inner : 2 * inner]
    value_rows = projected[:, 2 * inner :]
    query_heads = query_rows.reshape(slot_count, HEADS, HD)
    pieces = (
        lax.all_gather(key_rows, "space", axis=0, tiled=True),
        lax.all_gather(value_rows, "space", axis=0, tiled=True),
    )
    run_peak = jnp.full((HEADS, slot_count), -1e30, jnp.float32)
    key_part = pieces[0].reshape(pieces[0].shape[0], HEADS, HD)
    value_part = pieces[1].reshape(pieces[1].shape[0], HEADS, HD)
    scores = (
        jnp.einsum("qhd,khd->hqk", query_heads, key_part, preferred_element_type=jnp.float32)
        / root_size
    )
    new_peak = jnp.maximum(run_peak, jnp.max(scores, -1))
    weights = jnp.exp(scores - new_peak[..., None])
    run_total = jnp.sum(weights, -1)
    run_sum = jnp.einsum(
        "hqk,khd->hqd", weights.astype(jnp.bfloat16), value_part, preferred_element_type=jnp.float32
    )
    run_peak, run_total, run_sum = (new_peak, run_total, run_sum)
    attended = (
        (run_sum / run_total[..., None])
        .transpose(1, 0, 2)
        .reshape(slot_count, inner)
        .astype(jnp.bfloat16)
    )
    spatial_out = jnp.dot(attended, spatial_proj, preferred_element_type=jnp.float32).astype(
        jnp.bfloat16
    )
    spread_back = jnp.dot(one_hot, spatial_out, preferred_element_type=jnp.float32)
    after_spatial = (own_rows.astype(jnp.float32) + modulation[2] * spread_back).astype(
        jnp.bfloat16
    )
    by_place = lax.all_to_all(
        after_spatial[None], "frames", split_axis=1, concat_axis=0, tiled=True
    )
    frame_count = by_place.shape[0]
    place_count = by_place.shape[1]
    flat = by_place.reshape(frame_count * place_count, width)
    normed_time = modulate(flat, modulation, 3)
    projected_time = jnp.dot(normed_time, temporal_qkv, preferred_element_type=jnp.float32).astype(
        jnp.bfloat16
    )
    split = projected_time.reshape(frame_count, place_count, 3, HEADS, HD)
    scores_time = (
        jnp.einsum(
            "flhd,glhd->lhfg", split[:, :, 0], split[:, :, 1], preferred_element_type=jnp.float32
        )
        / root_size
    )
    weights_time = jnp.exp(scores_time - jnp.max(scores_time, -1, keepdims=True))
    total_time = jnp.sum(weights_time, -1)
    mixture_time = (
        jnp.einsum(
            "lhfg,glhd->flhd",
            weights_time.astype(jnp.bfloat16),
            split[:, :, 2],
            preferred_element_type=jnp.float32,
        )
        / total_time.transpose(2, 0, 1)[..., None]
    )
    attended_time = mixture_time.astype(jnp.bfloat16).reshape(frame_count * place_count, inner)
    branch = jnp.dot(attended_time, temporal_proj, preferred_element_type=jnp.float32)
    finished = (
        (flat.astype(jnp.float32) + modulation[5] * branch)
        .astype(jnp.bfloat16)
        .reshape(frame_count, place_count, width)
    )
    return lax.all_to_all(finished, "frames", split_axis=0, concat_axis=1, tiled=True)


def solution(mesh):
    placed = (P("frames", "space", None), P("frames", "space"), P(), P(), P(), P(), P())
    return jax.shard_map(
        shards, mesh=mesh, in_specs=placed, out_specs=P("frames", "space", None), check_vma=False
    )
```

profile of v0, /device:TPU:2, one launch (start us, length us, event | category | flops | bytes accessed | tf_op | source)
XLA Modules:
  0.0 201.5 jit_solution(2372403140848422935)
XLA Ops:
  6.5 0.0 copy-start
  6.5 0.0 copy-start.2
  6.5 0.0 all-gather.3.cloned.1.call-start
  6.5 1.8 slice_reduce_fusion.1
  8.3 0.7 broadcast_subtract_fusion
  9.0 0.1 convert_reduce_fusion.2
  9.2 1.4 convert_reduce_fusion.1
  10.6 1.6 fusion.16
  12.2 0.0 copy-done.2
  12.3 4.1 %convolution_convert_fusion.2 = bf16[224,1728]{1,0:T(8,128)(2,1)S(1)} fusion(bf16[1152,1728]{0,1:T(8,128)(2,1)} %param.10, bf16[1,448,1152]{2,1,0:T(8,128)(2,1)S(1)} %copy-done.2, f32[1152]{0:T(1024)S(1)} %get-tuple-element.6, f32[1152]{0:T(1024)S(1)} %get-tuple-element.7, f32[448]{0:T(512)S(1)} %add_rsqrt_fusion.1, f32[448]{0:T(512)S(1)} %broadcast_multiply_fusion.1, ...), kind=kOutput, calls=%fused_computation.24 | convolution fusion | flops 1127124992 | bytes 5803136 | tf_op jit(solution)/shard_map/dot_general | solution.py:41
  16.4 0.9 fusion.62
  17.3 0.0 all-gather.3.cloned.1.call-update
  17.3 0.0 all-gather.5.cloned.1.call-start
  17.4 0.7 all-gather.5.cloned.1.call-update
  18.1 0.9 copy.33
  18.9 39.3 %all-gather.3.cloned.1.call-done = bf16[1792,576]{1,0:T(8,128)(2,1)} async-done(((bf16[224,576]{1,0:T(8,128)(2,1)}), bf16[1792,576]{1,0:T(8,128)(2,1)}) %all-gather.3.cloned.1.call-update) | async-done | bytes 2064400 | tf_op jit(solution)/shard_map/all_gather | solution.py:49
  58.2 3.0 %copy.34 = bf16[1792,576]{0,1:T(8,128)(2,1)S(1)} copy(bf16[1792,576]{1,0:T(8,128)(2,1)} %all-gather.3.cloned.1.call-done) | data formatting | bytes 4128768 | tf_op jit(solution)/shard_map/all_gather | solution.py:49
  61.2 2.9 %multiply_reduce_fusion = (f32[8,224]{1,0:T(8,128)S(1)}, f32[8,224,1792]{2,1,0:T(8,128)S(1)}) fusion(bf16[224,8,72]{0,2,1:T(8,128)(2,1)} %bitcast.87, bf16[1792,8,72]{0,2,1:T(8,128)(2,1)S(1)} %bitcast.83), kind=kOutput, calls=%fused_computation.1 | convolution fusion | flops 468842752 | bytes 15174656 | tf_op jit(solution)/shard_map/qhd,khd->hqk/dot_general | solution.py:56
  64.2 0.0 copy-start.1
  64.2 4.6 %copy-done.1 = f32[8,224,1792]{2,1,0:T(8,128)} copy-done((f32[8,224,1792]{2,1,0:T(8,128)}, f32[8,224,1792]{2,1,0:T(8,128)S(1)}, u32[]{:S(2)}) %copy-start.1) | copy-done | bytes 12845080
  68.8 2.3 %fusion = f32[8,224]{1,0:T(8,128)S(1)} fusion(f32[8,224,1792]{2,1,0:T(8,128)S(1)} %get-tuple-element.20, f32[8,224]{1,0:T(8,128)S(1)} %broadcast_maximum_fusion), kind=kLoop, calls=%fused_computation.2 | loop fusion | flops 9632000 | bytes 12859392 | tf_op jit(solution)/shard_map/reduce_sum | solution.py:61
  71.1 24.5 %all-gather.5.cloned.1.call-done = bf16[1792,576]{1,0:T(8,128)(2,1)} async-done(((bf16[224,576]{1,0:T(8,128)(2,1)}), bf16[1792,576]{1,0:T(8,128)(2,1)}) %all-gather.5.cloned.1.call-update) | async-done | bytes 2064400 | tf_op jit(solution)/shard_map/all_gather | solution.py:50
  95.6 4.1 %copy.35 = bf16[1792,576]{0,1:T(8,128)(2,1)} copy(bf16[1792,576]{1,0:T(8,128)(2,1)} %all-gather.5.cloned.1.call-done) | data formatting | bytes 4128768 | tf_op jit(solution)/shard_map/all_gather | solution.py:50
  99.7 0.0 copy-start.3
  99.7 0.0 copy-start.8
  99.7 7.8 %fusion.45 = bf16[224,8,72]{0,2,1:T(8,128)(2,1)S(1)} fusion(bf16[1792,8,72]{0,2,1:T(8,128)(2,1)} %bitcast.86, f32[8,224,1792]{2,1,0:T(8,128)} %copy-done.1, f32[8,224]{1,0:T(8,128)S(1)} %broadcast_maximum_fusion, f32[224,8]{0,1:T(8,128)S(1)} %bitcast.89), kind=kOutput, calls=%fused_computation.54 | convolution fusion | flops 472313856 | bytes 15181824 | tf_op jit(solution)/shard_map/hqk,khd->hqd/dot_general | solution.py:62
  107.5 0.0 copy-done
  107.5 0.0 copy-done.3
  107.5 0.0 copy-done.8
  107.5 2.0 fusion.10
  109.5 2.8 %copy.59 = bf16[1,448,1152]{2,0,1:T(2,128)(2,1)S(1)} copy(bf16[1,448,1152]{2,1,0:T(8,128)(2,1)} %fusion.10) | data formatting | bytes 2064384 | tf_op jit(solution)/shard_map/broadcast_in_dim | solution.py:80
  112.3 0.6 broadcast.86
  112.9 7.9 %reduce.17 = bf16[448,1152]{1,0:T(8,128)(2,1)} reduce(bf16[448,1,1152]{2,1,0:T(2,128)(2,1)S(1)} %bitcast.84, bf16[]{:T(256)} %broadcast.86), dimensions={1}, to_apply=%bitcast.82.reduce_sub_computation | reduce | bytes 2064386
  120.8 2.5 %reshape.108 = bf16[32,2,8064]{2,1,0:T(2,128)(2,1)S(1)} reshape(bf16[448,1152]{1,0:T(8,128)(2,1)} %reduce.17) | data formatting | bytes 2064384
  123.3 23.9 %all_to_all.21 = bf16[32,2,8064]{2,1,0:T(2,128)(2,1)} all-to-all(bf16[32,2,8064]{2,1,0:T(2,128)(2,1)S(1)} %reshape.108), channel_id=1, replica_groups=mesh['frames'=32,'space'=8] {'frames'}, dimensions={0} | all-to-all | bytes 2064384 | tf_op jit(solution)/shard_map/all_to_all | solution.py:79
  147.2 4.2 %reshape.109 = bf16[448,1,1152]{2,1,0:T(2,128)(2,1)S(1)} reshape(bf16[32,2,8064]{2,1,0:T(2,128)(2,1)} %all_to_all.21) | data formatting | bytes 2064384
  151.4 0.0 copy-start.6
  151.4 0.0 copy-start.7
  151.4 0.0 copy-start.9
  151.4 0.2 convert_reduce_fusion
  151.6 0.0 copy-start.4
  151.6 0.4 fusion.25
  152.1 0.5 copy-done.4
  152.6 0.0 copy-done.6
  152.6 0.0 copy-done.7
  152.6 1.3 copy-done.9
  153.9 2.4 %convolution_convert_fusion = bf16[448,1728]{1,0:T(8,128)(2,1)S(1)} fusion(bf16[1152,1728]{0,1:T(8,128)(2,1)S(1)} %copy-done.9, bf16[1,448,1152]{2,1,0:T(8,128)(2,1)S(1)} %get-tuple-element.12, f32[1152]{0:T(1024)S(1)} %copy-done.6, f32[1152]{0:T(1024)S(1)} %copy-done.7, f32[448]{0:T(512)S(1)} %add_rsqrt_fusion, f32[448]{0:T(512)S(1)} %broadcast_multiply_fusion), kind=kOutput, calls=%fused_computation.14 | convolution fusion | flops 1787498496 | bytes 6574592 | tf_op jit(solution)/shard_map/dot_general | solution.py:86
  156.3 4.0 %reshape.98 = bf16[32,14,3,8,72]{4,3,2,1,0:T(8,128)(2,1)} reshape(bf16[448,1728]{1,0:T(8,128)(2,1)S(1)} %convolution_convert_fusion) | data formatting | bytes 3096576 | tf_op jit(solution)/shard_map/reshape | solution.py:89
  160.3 1.9 fusion.61
  162.2 0.6 multiply_reduce_fusion.1
  162.9 0.6 fusion.27
  163.5 1.1 fusion.26
  164.6 0.0 copy-start.5
  164.6 0.4 copy.42
  164.9 1.5 reshape.99
  166.5 0.0 copy-done.5
  166.5 2.5 %fusion.8 = bf16[448,1152]{1,0:T(8,128)(2,1)S(1)} fusion(bf16[448,576]{1,0:T(8,128)(2,1)} %reshape.99, bf16[576,1152]{1,0:T(8,128)(2,1)} %param.13, bf16[1,448,1152]{2,1,0:T(8,128)(2,1)S(1)} %copy-done.5, f32[1152]{0:T(1024)S(1)} %get-tuple-element.5), kind=kOutput, calls=%fused_computation.15 | convolution fusion | flops 596606976 | bytes 3912192 | tf_op jit(solution)/shard_map/dot_general | solution.py:108
  169.0 0.3 reshape.100
  169.4 23.1 %all_to_all.22 = bf16[32,14,1152]{2,1,0:T(8,128)(2,1)} all-to-all(bf16[32,14,1152]{2,1,0:T(8,128)(2,1)S(1)} %reshape.100), channel_id=1, replica_groups=mesh['frames'=32,'space'=8] {'frames'}, dimensions={0} | all-to-all | bytes 2064384 | tf_op jit(solution)/shard_map/all_to_all | solution.py:114
  192.5 2.2 %all_to_all.8 = bf16[1,448,1152]{2,1,0:T(8,128)(2,1)} reshape(bf16[32,14,1152]{2,1,0:T(8,128)(2,1)} %all_to_all.22) | data formatting | bytes 2064384 | tf_op jit(solution)/shard_map/all_to_all | solution.py:114
  (5 shorter events, 0.0 us)
Async XLA Ops:
  6.5 100.9 %copy-start = (bf16[576,1152]{1,0:T(8,128)(2,1)S(1)}, bf16[576,1152]{1,0:T(8,128)(2,1)}, u32[]{:S(2)}) copy-start(bf16[576,1152]{1,0:T(8,128)(2,1)} %param.11) | copy-start | bytes 3981316
  6.5 5.7 %copy-start.2 = (bf16[1,448,1152]{2,1,0:T(8,128)(2,1)S(1)}, bf16[1,448,1152]{2,1,0:T(8,128)(2,1)}, u32[]{:S(2)}) copy-start(bf16[1,448,1152]{2,1,0:T(8,128)(2,1)} %param.7) | copy-start | bytes 3096580
  6.5 51.7 %all-gather.3.cloned.1.call-start = ((), (), s32[]{:S(2)}) async-start(), calls=%async_computation.2 | async-start | bytes 2580480 | tf_op jit(solution)/shard_map/all_gather | solution.py:49
  17.3 78.2 %all-gather.5.cloned.1.call-start = ((), (), s32[]{:S(2)}) async-start(), calls=%async_computation.3 | async-start | bytes 2580480 | tf_op jit(solution)/shard_map/all_gather | solution.py:50
  64.2 4.6 %copy-start.1 = (f32[8,224,1792]{2,1,0:T(8,128)}, f32[8,224,1792]{2,1,0:T(8,128)S(1)}, u32[]{:S(2)}) copy-start(f32[8,224,1792]{2,1,0:T(8,128)S(1)} %get-tuple-element.20) | copy-start | bytes 38535172
  99.7 7.8 %copy-start.3 = (bf16[1,448,1152]{2,1,0:T(8,128)(2,1)S(1)}, bf16[1,448,1152]{2,1,0:T(8,128)(2,1)}, u32[]{:S(2)}) copy-start(bf16[1,448,1152]{2,1,0:T(8,128)(2,1)} %param.7) | copy-start | bytes 3096580
  99.7 7.8 %copy-start.8 = (f32[1152]{0:T(1024)S(1)}, f32[1152]{0:T(1024)}, u32[]{:S(2)}) copy-start(f32[1152]{0:T(1024)} %get-tuple-element.8) | copy-start | bytes 13828
  151.4 1.2 copy-start.6
  151.4 1.2 copy-start.7
  151.4 2.5 %copy-start.9 = (bf16[1152,1728]{0,1:T(8,128)(2,1)S(1)}, bf16[1152,1728]{0,1:T(8,128)(2,1)}, u32[]{:S(2)}) copy-start(bf16[1152,1728]{0,1:T(8,128)(2,1)} %param.12) | copy-start | bytes 11943940
  151.6 1.0 copy-start.4
  164.6 1.9 copy-start.5
Sparse Core Ops, SparseCore 0:
  17.4 40.7 all-gather.2
  60.1 35.4 all-gather.4
where the time goes:
time: 202 us; the launch traced here: 201 us
  waiting for transfers between devices  64.5 us (32%)
  blocking collectives  47 us (23%)
  local copies, waits for them, and re-layouts  35.6 us (18%)
  matrix products  23.5 us (12%)
  other arithmetic  17.2 us (9%)
  between operations  13.6 us (7%)
    all_gather x1, waiting for transfers between devices, shards(): lax.all_gather(key_rows, 'space', axis=0, tiled=True)  39.3 us
    all_gather x1, waiting for transfers between devices, shards(): lax.all_gather(value_rows, 'space', axis=0, tiled=True)  24.5 us
    all_to_all x1, blocking collectives, shards(): lax.all_to_all(after_spatial[None], 'frames', split_axis=1, concat_axis=0...  23.9 us
    all_to_all x1, blocking collectives, shards(): lax.all_to_all(finished, 'frames', split_axis=0, concat_axis=1, tiled=True)  23.1 us
    unnamed x23, local copies, waits for them, and re-layouts  13.7 us
    unnamed x1, other arithmetic  7.93 us
    dot_general x1, matrix products, shards(): jnp.einsum('hqk,khd->hqd', weights.astype(jnp.bfloat16), value_part, pref...  7.79 us
    all_gather x1, local copies, waits for them, and re-layouts, shards(): lax.all_gather(value_rows, 'space', axis=0, tiled=True)  4.13 us
  transfers between devices with their start and end apart: 2, of which 2 were waited for; matrix products, arithmetic and copies ran while one was open for 5% of the time, Pallas kernels for 0%

commit v1 on v0

--- a/solution.py
+++ b/solution.py
@@ -6,6 +6,11 @@
 
 HEADS = 8
 HD = 72
+
+
+def swapped_in(value, mesh_axis, along):
+    sent = jnp.stack([value] * lax.axis_size(mesh_axis))
+    return jnp.concatenate(lax.all_to_all(sent, mesh_axis, 0, 0), axis=along)
 
 
 def layer_norm(values):
@@ -47,7 +52,7 @@
     query_heads = query_rows.reshape(slot_count, HEADS, HD)
     pieces = (
         lax.all_gather(key_rows, "space", axis=0, tiled=True),
-        lax.all_gather(value_rows, "space", axis=0, tiled=True),
+        swapped_in(value_rows, "space", 0),
     )
     run_peak = jnp.full((HEADS, slot_count), -1e30, jnp.float32)
     key_part = pieces[0].reshape(pieces[0].shape[0], HEADS, HD)

time: 202 us -> 217 us (1.074); the launches traced: 201 us -> 214 us
  starting transfers between devices: 0.04 us -> 8.51 us
  blocking collectives: 47 us -> 40.4 us
  waiting for transfers between devices: 64.5 us -> 70.3 us
  local copies, waits for them, and re-layouts: 35.6 us -> 41.1 us
    all_to_all x0 -> x1, waiting for transfers between devices: none -> 69.6 us  [swapped_in(): return jnp.concatenate(lax.all_to_all(sent, mesh_axis, 0, 0), axis=along)]
    all_gather x1, waiting for transfers between devices: 39.3 us -> 0.01 us  [shards(): lax.all_gather(key_rows, 'space', axis=0, tiled=True)]
    all_gather x1 -> x0, waiting for transfers between devices: 24.5 us -> none  [shards(): lax.all_gather(value_rows, 'space', axis=0, tiled=True)]
    all_to_all x0 -> x1, starting transfers between devices: none -> 8.47 us  [swapped_in(): return jnp.concatenate(lax.all_to_all(sent, mesh_axis, 0, 0), axis=along)]
    another operation x0 -> x2, local copies, waits for them, and re-layouts: none -> 6.92 us  [the longest x1 5.35 us: shards(): value_part = pieces[1].reshape(pieces[1].shape[0], HEADS, HD)]
    all_to_all x0 -> x1, local copies, waits for them, and re-layouts: none -> 4.81 us  [swapped_in(): return jnp.concatenate(lax.all_to_all(sent, mesh_axis, 0, 0), axis=along)]
    all_to_all x1, blocking collectives: 23.1 us -> 18.5 us  [shards(): lax.all_to_all(finished, 'frames', split_axis=0, concat_axis=1, tiled=True)]
    all_gather x1 -> x0, local copies, waits for them, and re-layouts: 4.13 us -> none  [shards(): lax.all_gather(value_rows, 'space', axis=0, tiled=True)]
  transfers between devices with their start and end apart: 2 -> 2, of which waited for: 2 -> 1; matrix products, arithmetic and copies ran while one was open for 5% -> 5% of each run, Pallas kernels for 0% -> 0%
where the time goes in v1:
time: 217 us; the launch traced here: 214 us
  waiting for transfers between devices  70.3 us (32%)
  local copies, waits for them, and re-layouts  41.1 us (19%)
  blocking collectives  40.4 us (19%)
  matrix products  23.5 us (11%)
  other arithmetic  16.6 us (8%)
  between operations  13.6 us (6%)
  starting transfers between devices  8.51 us (4%)
    all_to_all x1, waiting for transfers between devices, swapped_in(): return jnp.concatenate(lax.all_to_all(sent, mesh_axis, 0, 0), axis=along)  69.6 us
    all_to_all x1, blocking collectives, shards(): lax.all_to_all(after_spatial[None], 'frames', split_axis=1, concat_axis=0...  22 us
    all_to_all x1, blocking collectives, shards(): lax.all_to_all(finished, 'frames', split_axis=0, concat_axis=1, tiled=True)  18.5 us
    unnamed x25, local copies, waits for them, and re-layouts  11.4 us
    all_to_all x1, starting transfers between devices, swapped_in(): return jnp.concatenate(lax.all_to_all(sent, mesh_axis, 0, 0), axis=along)  8.47 us
    unnamed x1, other arithmetic  8.15 us
    dot_general x1, matrix products, shards(): jnp.einsum('hqk,khd->hqd', weights.astype(jnp.bfloat16), value_part, pref...  7.78 us
    another operation x1, local copies, waits for them, and re-layouts, shards(): value_part = pieces[1].reshape(pieces[1].shape[0], HEADS, HD)  5.35 us
  transfers between devices with their start and end apart: 2, of which 1 were waited for; matrix products, arithmetic and copies ran while one was open for 5% of the time, Pallas kernels for 0%

profile of v1, /device:TPU:2, one launch (start us, length us, event | category | flops | bytes accessed | tf_op | source)
XLA Modules:
  0.0 214.1 jit_solution(2839947630310181183)
XLA Ops:
  6.5 0.0 copy-start
  6.5 0.0 copy-start.2
  6.5 0.0 copy-start.9
  6.5 1.7 slice_reduce_fusion.1
  8.2 1.4 convert_reduce_fusion.1
  9.7 1.6 fusion.16
  11.3 0.0 copy-done.9
  11.4 0.1 convert_reduce_fusion.2
  11.5 0.0 copy-done.2
  11.5 4.1 %convolution_convert_fusion.2 = bf16[224,1728]{1,0:T(8,128)(2,1)S(1)} fusion(bf16[1152,1728]{0,1:T(8,128)(2,1)} %param.10, bf16[1,448,1152]{2,1,0:T(8,128)(2,1)S(1)} %copy-done.2, f32[1152]{0:T(1024)S(1)} %get-tuple-element.6, f32[1152]{0:T(1024)S(1)} %get-tuple-element.7, f32[448]{0:T(512)S(1)} %add_rsqrt_fusion.1, f32[448]{0:T(512)S(1)} %broadcast_multiply_fusion.1, ...), kind=kOutput, calls=%fused_computation.24 | convolution fusion | flops 1127124992 | bytes 5803136 | tf_op jit(solution)/shard_map/dot_general | solution.py:46
  15.6 0.9 fusion.62
  16.5 1.6 stack.2
  18.1 8.5 %all-to-all-start = ((bf16[8,224,576]{2,1,0:T(8,128)(2,1)}), bf16[8,224,576]{2,1,0:T(8,128)(2,1)}, u32[]{:S(2)}, u32[]{:S(2)}) async-start(bf16[8,224,576]{2,1,0:T(8,128)(2,1)} %stack.2), calls=%async_computation | async-start | bytes 4587520 | tf_op jit(solution)/shard_map/all_to_all | solution.py:13
  26.5 0.0 all-gather.2.cloned.1.call-start
  26.6 0.7 all-gather.2.cloned.1.call-update
  27.3 0.9 copy.33
  28.1 69.6 %all-to-all-done = bf16[8,224,576]{2,1,0:T(8,128)(2,1)} async-done(((bf16[8,224,576]{2,1,0:T(8,128)(2,1)}), bf16[8,224,576]{2,1,0:T(8,128)(2,1)}, u32[]{:S(2)}, u32[]{:S(2)}) %all-to-all-start) | async-done | bytes 2064416 | tf_op jit(solution)/shard_map/all_to_all | solution.py:13
  97.8 4.8 %copy.35 = bf16[8,224,576]{1,0,2:T(8,128)(2,1)} copy(bf16[8,224,576]{2,1,0:T(8,128)(2,1)} %all-to-all-done) | data formatting | bytes 4128768 | tf_op jit(solution)/shard_map/all_to_all | solution.py:13
  102.6 5.4 %reshape_reshape.3 = bf16[1792,8,72]{0,2,1:T(8,128)(2,1)} reshape(bf16[8,224,576]{1,0,2:T(8,128)(2,1)} %copy.35) | data formatting | bytes 4128768 | tf_op jit(solution)/shard_map/reshape;reshape | solution.py:59
  107.9 0.0 all-gather.2.cloned.1.call-done
  107.9 3.2 %copy.34 = bf16[1792,576]{0,1:T(8,128)(2,1)S(1)} copy(bf16[1792,576]{1,0:T(8,128)(2,1)} %all-gather.2.cloned.1.call-done) | data formatting | bytes 4128768 | tf_op jit(solution)/shard_map/all_gather | solution.py:54
  111.1 2.9 %multiply_reduce_fusion = (f32[8,224]{1,0:T(8,128)S(1)}, f32[8,224,1792]{2,1,0:T(8,128)S(1)}) fusion(bf16[224,8,72]{0,2,1:T(8,128)(2,1)} %bitcast.87, bf16[1792,8,72]{0,2,1:T(8,128)(2,1)S(1)} %bitcast.84), kind=kOutput, calls=%fused_computation.1 | convolution fusion | flops 468842752 | bytes 15174656 | tf_op jit(solution)/shard_map/qhd,khd->hqk/dot_general | solution.py:61
  114.0 0.0 copy-start.1
  114.1 2.3 %fusion = f32[8,224]{1,0:T(8,128)S(1)} fusion(f32[8,224,1792]{2,1,0:T(8,128)S(1)} %get-tuple-element.20, f32[8,224]{1,0:T(8,128)S(1)} %broadcast_maximum_fusion), kind=kLoop, calls=%fused_computation.2 | loop fusion | flops 9632000 | bytes 12859392 | tf_op jit(solution)/shard_map/reduce_sum | solution.py:66
  116.3 2.3 %copy-done.1 = f32[8,224,1792]{2,1,0:T(8,128)} copy-done((f32[8,224,1792]{2,1,0:T(8,128)}, f32[8,224,1792]{2,1,0:T(8,128)S(1)}, u32[]{:S(2)}) %copy-start.1) | copy-done | bytes 12845080
  118.6 0.0 copy-start.3
  118.7 0.0 copy-start.8
  118.7 7.8 %fusion.45 = bf16[224,8,72]{0,2,1:T(8,128)(2,1)S(1)} fusion(bf16[1792,8,72]{0,2,1:T(8,128)(2,1)} %reshape_reshape.3, f32[8,224,1792]{2,1,0:T(8,128)} %copy-done.1, f32[8,224]{1,0:T(8,128)S(1)} %broadcast_maximum_fusion, f32[224,8]{0,1:T(8,128)S(1)} %bitcast.89), kind=kOutput, calls=%fused_computation.54 | convolution fusion | flops 472313856 | bytes 15181824 | tf_op jit(solution)/shard_map/hqk,khd->hqd/dot_general | solution.py:67
  126.4 0.0 copy-done
  126.4 0.0 copy-done.3
  126.5 0.0 copy-done.8
  126.5 2.0 fusion.10
  128.4 2.8 %copy.59 = bf16[1,448,1152]{2,0,1:T(2,128)(2,1)S(1)} copy(bf16[1,448,1152]{2,1,0:T(8,128)(2,1)} %fusion.10) | data formatting | bytes 2064384 | tf_op jit(solution)/shard_map/broadcast_in_dim | solution.py:85
  131.2 0.6 broadcast.88
  131.8 8.2 %reduce.17 = bf16[448,1152]{1,0:T(8,128)(2,1)} reduce(bf16[448,1,1152]{2,1,0:T(2,128)(2,1)S(1)} %bitcast.85, bf16[]{:T(256)} %broadcast.88), dimensions={1}, to_apply=%bitcast.83.reduce_sub_computation | reduce | bytes 2064386
  140.0 2.4 %reshape.106 = bf16[32,2,8064]{2,1,0:T(2,128)(2,1)S(1)} reshape(bf16[448,1152]{1,0:T(8,128)(2,1)} %reduce.17) | data formatting | bytes 2064384
  142.4 22.0 %all_to_all.26 = bf16[32,2,8064]{2,1,0:T(2,128)(2,1)} all-to-all(bf16[32,2,8064]{2,1,0:T(2,128)(2,1)S(1)} %reshape.106), channel_id=1, replica_groups=mesh['frames'=32,'space'=8] {'frames'}, dimensions={0} | all-to-all | bytes 2064384 | tf_op jit(solution)/shard_map/all_to_all | solution.py:84
  164.4 4.2 %reshape.107 = bf16[448,1,1152]{2,1,0:T(2,128)(2,1)S(1)} reshape(bf16[32,2,8064]{2,1,0:T(2,128)(2,1)} %all_to_all.26) | data formatting | bytes 2064384
  168.6 0.0 copy-start.6
  168.6 0.0 copy-start.7
  168.6 0.0 copy-start.10
  168.6 0.2 convert_reduce_fusion
  168.9 0.0 copy-start.4
  168.9 0.4 fusion.25
  169.3 0.5 copy-done.4
  169.8 0.0 copy-done.6
  169.8 0.0 copy-done.7
  169.8 1.3 copy-done.10
  171.1 2.5 %convolution_convert_fusion = bf16[448,1728]{1,0:T(8,128)(2,1)S(1)} fusion(bf16[1152,1728]{0,1:T(8,128)(2,1)S(1)} %copy-done.10, bf16[1,448,1152]{2,1,0:T(8,128)(2,1)S(1)} %get-tuple-element.12, f32[1152]{0:T(1024)S(1)} %copy-done.6, f32[1152]{0:T(1024)S(1)} %copy-done.7, f32[448]{0:T(512)S(1)} %add_rsqrt_fusion, f32[448]{0:T(512)S(1)} %broadcast_multiply_fusion), kind=kOutput, calls=%fused_computation.14 | convolution fusion | flops 1787498496 | bytes 6574592 | tf_op jit(solution)/shard_map/dot_general | solution.py:91
  173.6 4.0 %reshape.96 = bf16[32,14,3,8,72]{4,3,2,1,0:T(8,128)(2,1)} reshape(bf16[448,1728]{1,0:T(8,128)(2,1)S(1)} %convolution_convert_fusion) | data formatting | bytes 3096576 | tf_op jit(solution)/shard_map/reshape | solution.py:94
  177.6 1.9 fusion.61
  179.5 0.6 multiply_reduce_fusion.1
  180.1 0.6 fusion.27
  180.7 1.1 fusion.26
  181.8 0.0 copy-start.5
  181.8 0.4 copy.42
  182.2 1.5 reshape.97
  183.7 0.0 copy-done.5
  183.7 2.5 %fusion.8 = bf16[448,1152]{1,0:T(8,128)(2,1)S(1)} fusion(bf16[448,576]{1,0:T(8,128)(2,1)} %reshape.97, bf16[576,1152]{1,0:T(8,128)(2,1)} %param.13, bf16[1,448,1152]{2,1,0:T(8,128)(2,1)S(1)} %copy-done.5, f32[1152]{0:T(1024)S(1)} %get-tuple-element.5), kind=kOutput, calls=%fused_computation.15 | convolution fusion | flops 596606976 | bytes 3912192 | tf_op jit(solution)/shard_map/dot_general | solution.py:113
  186.3 0.3 reshape.98
  186.6 18.5 %all_to_all.27 = bf16[32,14,1152]{2,1,0:T(8,128)(2,1)} all-to-all(bf16[32,14,1152]{2,1,0:T(8,128)(2,1)S(1)} %reshape.98), channel_id=1, replica_groups=mesh['frames'=32,'space'=8] {'frames'}, dimensions={0} | all-to-all | bytes 2064384 | tf_op jit(solution)/shard_map/all_to_all | solution.py:119
  205.1 2.2 %all_to_all.22 = bf16[1,448,1152]{2,1,0:T(8,128)(2,1)} reshape(bf16[32,14,1152]{2,1,0:T(8,128)(2,1)} %all_to_all.27) | data formatting | bytes 2064384 | tf_op jit(solution)/shard_map/all_to_all | solution.py:119
  (6 shorter events, 0.0 us)
Async XLA Ops:
  6.5 119.9 %copy-start = (bf16[576,1152]{1,0:T(8,128)(2,1)S(1)}, bf16[576,1152]{1,0:T(8,128)(2,1)}, u32[]{:S(2)}) copy-start(bf16[576,1152]{1,0:T(8,128)(2,1)} %param.11) | copy-start | bytes 3981316
  6.5 5.0 %copy-start.2 = (bf16[1,448,1152]{2,1,0:T(8,128)(2,1)S(1)}, bf16[1,448,1152]{2,1,0:T(8,128)(2,1)}, u32[]{:S(2)}) copy-start(bf16[1,448,1152]{2,1,0:T(8,128)(2,1)} %param.7) | copy-start | bytes 3096580
  6.5 4.8 %copy-start.9 = (s32[1,448]{1,0:T(1,128)S(1)}, s32[1,448]{1,0:T(1,128)}, u32[]{:S(2)}) copy-start(s32[1,448]{1,0:T(1,128)} %param.8) | copy-start | bytes 5380
  18.1 79.7 %all-to-all-start = ((bf16[8,224,576]{2,1,0:T(8,128)(2,1)}), bf16[8,224,576]{2,1,0:T(8,128)(2,1)}, u32[]{:S(2)}, u32[]{:S(2)}) async-start(bf16[8,224,576]{2,1,0:T(8,128)(2,1)} %stack.2), calls=%async_computation | async-start | bytes 4587520 | tf_op jit(solution)/shard_map/all_to_all | solution.py:13
  26.5 81.4 %all-gather.2.cloned.1.call-start = ((), (), s32[]{:S(2)}) async-start(), calls=%async_computation.3 | async-start | bytes 2580480 | tf_op jit(solution)/shard_map/all_gather | solution.py:54
  114.0 4.6 %copy-start.1 = (f32[8,224,1792]{2,1,0:T(8,128)}, f32[8,224,1792]{2,1,0:T(8,128)S(1)}, u32[]{:S(2)}) copy-start(f32[8,224,1792]{2,1,0:T(8,128)S(1)} %get-tuple-element.20) | copy-start | bytes 38535172
  118.6 7.8 %copy-start.3 = (bf16[1,448,1152]{2,1,0:T(8,128)(2,1)S(1)}, bf16[1,448,1152]{2,1,0:T(8,128)(2,1)}, u32[]{:S(2)}) copy-start(bf16[1,448,1152]{2,1,0:T(8,128)(2,1)} %param.7) | copy-start | bytes 3096580
  118.7 7.8 %copy-start.8 = (f32[1152]{0:T(1024)S(1)}, f32[1152]{0:T(1024)}, u32[]{:S(2)}) copy-start(f32[1152]{0:T(1024)} %get-tuple-element.8) | copy-start | bytes 13828
  168.6 1.2 copy-start.6
  168.6 1.2 copy-start.7
  168.6 2.5 %copy-start.10 = (bf16[1152,1728]{0,1:T(8,128)(2,1)S(1)}, bf16[1152,1728]{0,1:T(8,128)(2,1)}, u32[]{:S(2)}) copy-start(bf16[1152,1728]{0,1:T(8,128)(2,1)} %param.12) | copy-start | bytes 11943940
  168.9 1.0 copy-start.4
  181.8 1.9 copy-start.5
Sparse Core Ops, SparseCore 0:
  29.2 69.5 all-gather.1
